TPU v7x, 128 devices: a whole 4x4x4 slice. The times are simulated.
128 devices in a mesh: wide: 16 (over z, x_lo, core), tall: 8 (over x_hi, y).
Axes of the slice: x: 4 (x_hi: 2, x_lo: 2; x = x_hi * 2 + x_lo), y: 4, z: 4, core: 2. Of those that a mesh axis runs over, the one named last changes fastest.
Arguments:
- initial: float32 [16384, 16384], P(('wide', 'tall')), as said below
- child_tiles: float32 [8192, 128, 128], P(('wide', 'tall')), may hold values from -0.75 to 0.75
- child_targets: int32 [8192, 2], P(('wide', 'tall')), may hold values from 0 to 127, as said below
Outputs:
- front: float32 [16384, 16384], P('tall', 'wide')
Inputs may be any that keep to these rules, and one draw needn't show every extreme that they name: initial is symmetric, and assembled with its lower triangle mirrored is positive definite. `child_targets`: tile t * 8 + k of a device (t < 8, k < 8) lands on a block whose rows lie in the 128 rows of initial held by device g * 8 + t, g being the sender's index along wide; such a block's grid owner is the device at tall index (block row * 1) mod 8 and wide index (block column * 128 // 512) mod 16; the 8 tiles of one device with the same t go to 8 different grid owners, so one device sends at most one tile to one owner; in every grid row some owner gets one tile from every device.
All inputs are finite; a program needn't handle non-finite values.
Results may differ from a plain program's by a relative error of at most 0.0003.
Values sent between devices are 32-bit elements; how exact they have to be, the bound alone decides.
A program may use at most 192 MiB of HBM per device.

v0:
```python
import jax
import jax.numpy as jnp
import numpy as np
from jax import lax
from jax.sharding import PartitionSpec as P

PANEL = 512
PANELS = 2
full_precision = lax.Precision.HIGHEST


def from_root(value, axis, source):
    kept = jnp.where(lax.axis_index(axis) == source, value, 0).astype(value.dtype)
    return lax.psum(kept, axis)


def add_blocks(base, tiles, block_index, tile_edge):
    base_rows, base_cols = base.shape
    row_count = base_rows // tile_edge
    col_count = base_cols // tile_edge
    slot_ids = jnp.arange(row_count * col_count, dtype=jnp.int32)
    selector = (slot_ids[:, None] == block_index[None, :]).astype(jnp.float32)
    summed = jnp.dot(selector, tiles, precision=full_precision, preferred_element_type=jnp.float32)
    summed = summed.reshape(row_count, col_count, tile_edge, tile_edge).transpose(0, 2, 1, 3)
    return base + summed.reshape(base_rows, base_cols)


def relayout(slab, wide_size, panel_width):
    slab_rows, front_order = slab.shape
    col_tiles = front_order // (panel_width * wide_size)
    pieces_out = slab.reshape(slab_rows, col_tiles, wide_size, panel_width)
    arrived = lax.all_to_all(pieces_out, "wide", split_axis=2, concat_axis=0, tiled=True)
    return arrived.reshape(wide_size * slab_rows, col_tiles * panel_width)


def share_strip(front_local, panel_at, panel_width):
    wide_size = lax.axis_size("wide")
    home_tile = panel_at // wide_size
    column_piece = lax.slice_in_dim(
        front_local, home_tile * panel_width, (home_tile + 1) * panel_width, axis=1
    )
    return from_root(column_piece, "wide", panel_at % wide_size)


def block_tables(wanted, tall_size):
    owners = wanted % tall_size
    slots_at = wanted // tall_size
    width_wanted = wanted.shape[1]
    same_owner = owners[:, :, None] == owners[:, None, :]
    earlier = np.tril(np.ones((width_wanted, width_wanted), dtype=np.int32), -1)[None, :, :] > 0
    ranks = np.sum(same_owner & earlier, axis=2)
    piece_depth = int(np.max(ranks)) + 1
    talls = np.arange(tall_size)
    places = np.arange(piece_depth)
    matches = (owners[:, None, None, :] == talls[None, :, None, None]) & (
        ranks[:, None, None, :] == places[None, None, :, None]
    )
    senders = np.sum(matches * slots_at[:, None, None, :], axis=3).astype(np.int32)
    receivers = (owners * piece_depth + ranks).astype(np.int32)
    return (senders, receivers)


def owned_piece(source, senders, group_at, tall_at, slab_rows):
    slot_count = source.shape[0] // slab_rows
    blocks = source.reshape(slot_count, slab_rows, source.shape[1])
    chosen = jnp.asarray(senders)[group_at, tall_at]
    return jnp.take(blocks, chosen, axis=0)


def order_rows(gathered, receivers, group_at):
    placed = jnp.take(gathered, jnp.asarray(receivers)[group_at], axis=0)
    return placed.reshape(placed.shape[0] * placed.shape[1], placed.shape[2])


def body(initial, child_tiles, child_targets):
    wide_size = lax.axis_size("wide")
    tall_size = lax.axis_size("tall")
    wide_at = lax.axis_index("wide")
    tall_at = lax.axis_index("tall")
    slab_rows, front_order = initial.shape
    tile_count, tile_edge, _ = child_tiles.shape
    per_row = tile_count // tall_size
    panel_width = PANEL
    col_tiles = front_order // (panel_width * wide_size)
    blocks_per_panel = panel_width // slab_rows
    flat_tiles = child_tiles.reshape(tile_count, tile_edge * tile_edge)
    front_local = relayout(initial, wide_size, panel_width)
    target_wide = child_targets[:, 1] * tile_edge // panel_width % wide_size
    target_tall = jnp.arange(tile_count, dtype=jnp.int32) // per_row
    target_slot = target_wide * tall_size + target_tall
    slot_ids = jnp.arange(wide_size * tall_size, dtype=jnp.int32)
    selector = slot_ids[:, None] == target_slot[None, :]
    buffer = jnp.dot(
        selector.astype(jnp.float32),
        flat_tiles,
        precision=full_precision,
        preferred_element_type=jnp.float32,
    )
    filled = jnp.any(selector, axis=1)
    placed = jnp.sum(selector.astype(jnp.int32)[:, :, None] * child_targets[None, :, :], axis=1)
    placed = jnp.where(filled[:, None], placed, -1)
    arrived, targets = (
        lax.all_to_all(buffer, ("wide", "tall"), split_axis=0, concat_axis=0, tiled=True),
        lax.all_to_all(placed, ("wide", "tall"), split_axis=0, concat_axis=0, tiled=True),
    )
    usable = targets[:, 0] >= 0
    row_global = targets[:, 0] * tile_edge
    row_group = row_global // slab_rows
    local_row = row_group // tall_size * slab_rows + row_global % slab_rows
    col_global = targets[:, 1] * tile_edge
    local_col = col_global // panel_width // wide_size * panel_width + col_global % panel_width
    grid_index = (
        local_row // tile_edge * (col_tiles * panel_width // tile_edge) + local_col // tile_edge
    )
    grid_index = jnp.where(usable, grid_index, -1)
    front_local = add_blocks(front_local, arrived, grid_index, tile_edge)
    local_index = jnp.arange(front_local.shape[0], dtype=jnp.int32)
    global_row = (
        local_index // slab_rows * tall_size + tall_at
    ) * slab_rows + local_index % slab_rows
    tile_steps = np.arange(col_tiles)
    inner_steps = np.arange(blocks_per_panel)
    wide_steps = np.arange(wide_size)
    solved_wanted = (
        (tile_steps[None, :, None] * wide_size + wide_steps[:, None, None]) * blocks_per_panel
        + inner_steps[None, None, :]
    ).reshape(wide_size, col_tiles * blocks_per_panel)
    solved_send, solved_receive = block_tables(solved_wanted, tall_size)
    identity = jnp.eye(panel_width, dtype=jnp.float32)
    column_strip = share_strip(front_local, 0, panel_width)
    for panel_at in range(PANELS):
        low_row = panel_at * panel_width
        high_row = low_row + panel_width
        diag_wanted = (np.arange(blocks_per_panel) + low_row // slab_rows)[None, :]
        diag_send, diag_receive = block_tables(diag_wanted, tall_size)
        diag_piece = owned_piece(column_strip, diag_send, 0, tall_at, slab_rows)
        diag_block = order_rows(
            lax.all_gather(diag_piece, "tall", axis=0, tiled=True), diag_receive, 0
        )
        factor = jnp.linalg.cholesky(jnp.tril(diag_block) + jnp.tril(diag_block, -1).T)
        inverse = lax.linalg.triangular_solve(factor, identity, left_side=True, lower=True)
        solved = jnp.dot(
            column_strip, inverse.T, precision=full_precision, preferred_element_type=jnp.float32
        )
        below_mask = (global_row >= high_row)[:, None]
        inside = ((global_row >= low_row) & (global_row < high_row))[:, None]
        lower_rows = jnp.where(below_mask, solved, 0.0)
        new_diag = jnp.tril(factor) + jnp.triu(diag_block, 1)
        diag_rows = jnp.take(new_diag, jnp.clip(global_row - low_row, 0, panel_width - 1), axis=0)
        new_strip = jnp.where(below_mask, solved, jnp.where(inside, diag_rows, column_strip))
        solved_piece = owned_piece(lower_rows, solved_send, wide_at, tall_at, slab_rows)
        column_rows = order_rows(
            lax.all_gather(solved_piece, "tall", axis=0, tiled=True), solved_receive, wide_at
        )
        root_wide = panel_at % wide_size
        home_tile = panel_at // wide_size
        has_next = panel_at + 1 < PANELS
        change = jnp.dot(
            lower_rows, column_rows.T, precision=full_precision, preferred_element_type=jnp.float32
        )
        front_local = front_local - change
        current = lax.slice_in_dim(
            front_local, home_tile * panel_width, (home_tile + 1) * panel_width, axis=1
        )
        front_local = front_local.at[
            :, home_tile * panel_width : (home_tile + 1) * panel_width
        ].set(jnp.where(wide_at == root_wide, new_strip, current))
        if has_next:
            column_strip = share_strip(front_local, panel_at + 1, panel_width)
    return front_local


def solution(mesh):
    return jax.shard_map(
        body,
        mesh=mesh,
        in_specs=(
            P(("wide", "tall"), None),
            P(("wide", "tall"), None, None),
            P(("wide", "tall"), None),
        ),
        out_specs=P("tall", "wide"),
        check_vma=False,
    )
```

profile of v0, /device:TPU:1, one launch (start us, length us, event | category | flops | bytes accessed | tf_op | source)
XLA Modules:
  0.0 1217.4 jit_solution(8326474147539438546)
XLA Ops:
  8.9 11.5 all-to-all-start.1
  20.4 9.9 copy.62
  30.2 9.5 copy.39
  39.7 6.5 all-to-all-start
  46.2 8.4 convolution_bitcast_fusion
  54.5 9.8 copy.41
  64.4 76.3 %all-to-all-done = f32[128,2,16,512]{3,1,0,2:T(2,128)} async-done(((f32[128,2,16,512]{3,1,0,2:T(2,128)}), f32[128,2,16,512]{3,1,0,2:T(2,128)}, u32[]{:S(2)}, u32[]{:S(2)}) %all-to-all-start) | async-done | bytes 8388640 | tf_op jit(solution)/shard_map/all_to_all | solution.py:32
  140.6 8.4 all-to-all-start.2
  149.5 8.9 copy.63
  158.3 90.6 %all-to-all-done.2 = f32[128,1,16384]{2,1,0:T(1,128)} async-done(((f32[128,1,16384]{2,1,0:T(1,128)}), f32[128,1,16384]{2,1,0:T(1,128)}, u32[]{:S(2)}, u32[]{:S(2)}) %all-to-all-start.2) | async-done | bytes 8388640 | tf_op jit(solution)/shard_map/all_to_all | solution.py:103
  248.9 18.0 %copy.61 = f32[128,1,16384]{0,2,1:T(8,128)} copy(f32[128,1,16384]{2,1,0:T(1,128)} %all-to-all-done.2) | data formatting | bytes 16777216 | tf_op jit(solution)/shard_map/dot_general | solution.py:23
  266.9 11.2 fusion.82
  278.1 12.3 %bitcast_add_fusion = f32[2048,1024]{1,0:T(8,128)} fusion(f32[2048,1024]{1,0:T(8,128)} %bitcast.181, f32[256,8,8,128]{3,2,1,0:T(8,128)} %bitcast.182), kind=kLoop, calls=%fused_computation.13 | loop fusion | flops 2097152 | bytes 25165824 | tf_op jit(solution)/shard_map/add | solution.py:25
  290.4 4.7 slice_select_fusion
  295.1 135.9 %all-reduce.4.cloned.1.call-done = f32[2048,512]{1,0:T(8,128)} async-done(((f32[2048,512]{1,0:T(8,128)}), f32[2048,512]{1,0:T(8,128)}) %all-reduce.4.cloned.1.call-update) | async-done | bytes 4194320 | tf_op jit(solution)/shard_map/psum | solution.py:14
  435.2 52.7 %all-gather.5.cloned.1.call-done = f32[8,128,512]{2,1,0:T(8,128)} async-done(((f32[1,128,512]{2,1,0:T(8,128)}), f32[8,128,512]{2,1,0:T(8,128)}) %all-gather.5.cloned.1.call-update) | async-done | bytes 2097168 | tf_op jit(solution)/shard_map/all_gather | solution.py:138
  487.9 2.2 gather_fusion
  496.7 11.7 cholesky.286
  508.6 9.8 custom-call.27
  520.9 11.9 cholesky.305
  532.8 9.8 custom-call.28
  544.2 11.7 cholesky.326
  555.9 9.8 custom-call.29
  567.2 11.9 cholesky.343
  583.8 2.4 fusion.25
  586.3 11.6 while.7
  587.0 2.2 bitcast_dynamic-update-slice_fusion.4
  589.9 2.2 bitcast_dynamic-update-slice_fusion.4
  592.8 2.2 bitcast_dynamic-update-slice_fusion.4
  595.7 2.2 bitcast_dynamic-update-slice_fusion.4
  597.8 39.3 %custom-call.30 = f32[4,128,128]{1,2,0:T(8,128)S(1)} custom-call(f32[4,128,128]{2,1,0:T(8,128)S(1)} %get-tuple-element.61), custom_call_target="InvertDiagBlocksLowerTriangular" | custom-call | tf_op jit(solution)/shard_map/triangular_solve/custom-call.3 | solution.py:141
  643.2 9.0 broadcast_select_fusion.2
  652.2 2.8 gather_fusion.1
  657.2 8.9 gather_fusion.3
  666.1 59.2 %all-gather.7.cloned.1.call-done = f32[16,128,512]{2,1,0:T(8,128)} async-done(((f32[2,128,512]{2,1,0:T(8,128)}), f32[16,128,512]{2,1,0:T(8,128)}) %all-gather.7.cloned.1.call-update) | async-done | bytes 4194320 | tf_op jit(solution)/shard_map/all_gather | solution.py:153
  725.3 2.9 gather_fusion.2
  728.5 1.9 copy-done.1
  730.4 17.0 %convolution_subtract_fusion.1 = f32[2048,1024]{1,0:T(8,128)S(1)} fusion(f32[2048,1024]{1,0:T(8,128)} %bitcast_add_fusion, f32[2048,512]{1,0:T(8,128)S(1)} %copy-done.1, f32[1024,512]{1,0:T(8,128)S(1)} %bitcast.191), kind=kOutput, calls=%fused_computation.25 | convolution fusion | flops 12886999040 | bytes 23068672 | tf_op jit(solution)/shard_map/dot_general | solution.py:158
  747.4 6.1 broadcast_select_fusion.1
  753.6 133.2 %all-reduce.6.cloned.1.call-done = f32[2048,512]{1,0:T(8,128)} async-done(((f32[2048,512]{1,0:T(8,128)}), f32[2048,512]{1,0:T(8,128)}) %all-reduce.6.cloned.1.call-update) | async-done | bytes 4194320 | tf_op jit(solution)/shard_map/psum | solution.py:14
  888.8 54.8 %all-gather.9.cloned.1.call-done = f32[8,128,512]{2,1,0:T(8,128)} async-done(((f32[1,128,512]{2,1,0:T(8,128)}), f32[8,128,512]{2,1,0:T(8,128)}) %all-gather.9.cloned.1.call-update) | async-done | bytes 2097168 | tf_op jit(solution)/shard_map/all_gather | solution.py:138
  943.6 2.2 gather_fusion.4
  952.6 11.7 cholesky.358
  964.5 9.8 custom-call.31
  976.9 11.7 cholesky.377
  988.6 10.0 custom-call.32
  1000.2 11.7 cholesky.398
  1011.9 9.8 custom-call.33
  1023.2 12.1 cholesky.415
  1040.4 2.5 fusion.22
  1042.9 10.8 while.8
  1043.5 2.1 bitcast_dynamic-update-slice_fusion.5
  1046.2 2.1 bitcast_dynamic-update-slice_fusion.5
  1048.9 2.1 bitcast_dynamic-update-slice_fusion.5
  1051.7 2.0 bitcast_dynamic-update-slice_fusion.5
  1053.7 39.3 %custom-call.34 = f32[4,128,128]{1,2,0:T(8,128)S(1)} custom-call(f32[4,128,128]{2,1,0:T(8,128)S(1)} %get-tuple-element.62), custom_call_target="InvertDiagBlocksLowerTriangular" | custom-call | tf_op jit(solution)/shard_map/triangular_solve/custom-call.3 | solution.py:141
  1099.1 8.9 broadcast_select_fusion
  1108.0 2.8 gather_fusion.5
  1111.8 4.6 constant_dynamic-update-slice_fusion.6
  1116.4 8.9 gather_fusion.7
  1125.3 55.8 %all-gather.11.cloned.1.call-done = f32[16,128,512]{2,1,0:T(8,128)} async-done(((f32[2,128,512]{2,1,0:T(8,128)}), f32[16,128,512]{2,1,0:T(8,128)}) %all-gather.11.cloned.1.call-update) | async-done | bytes 4194320 | tf_op jit(solution)/shard_map/all_gather | solution.py:153
  1181.1 2.9 gather_fusion.6
  1186.2 17.8 %convolution_subtract_fusion = f32[2048,1024]{1,0:T(8,128)} fusion(f32[2048,1024]{1,0:T(8,128)} %constant_dynamic-update-slice_fusion.6, f32[2048,512]{1,0:T(8,128)S(1)} %copy-done.2, f32[1024,512]{1,0:T(8,128)S(1)} %bitcast.190), kind=kOutput, calls=%fused_computation.24 | convolution fusion | flops 12886999040 | bytes 23068672 | tf_op jit(solution)/shard_map/dot_general | solution.py:158
  1203.9 6.4 fusion
  (154 shorter events, 61.2 us)
Async XLA Ops:
  8.9 30.9 %all-to-all-start.1 = ((s32[128,1,2]{2,1,0:T(1,128)}), s32[128,1,2]{2,1,0:T(1,128)S(1)}, u32[]{:S(2)}, u32[]{:S(2)}) async-start(s32[128,1,2]{2,1,0:T(1,128)} %copy.40), calls=%async_computation.1 | async-start | bytes 131072 | tf_op jit(solution)/shard_map/all_to_all | solution.py:104
  39.7 100.9 %all-to-all-start = ((f32[128,2,16,512]{3,1,0,2:T(2,128)}), f32[128,2,16,512]{3,1,0,2:T(2,128)}, u32[]{:S(2)}, u32[]{:S(2)}) async-start(f32[128,2,16,512]{3,1,0,2:T(2,128)} %copy.39), calls=%async_computation | async-start | bytes 16777216 | tf_op jit(solution)/shard_map/all_to_all | solution.py:32
  140.6 108.2 %all-to-all-start.2 = ((f32[128,1,16384]{2,1,0:T(1,128)}), f32[128,1,16384]{2,1,0:T(1,128)}, u32[]{:S(2)}, u32[]{:S(2)}) async-start(f32[128,1,16384]{2,1,0:T(1,128)} %copy.41), calls=%async_computation.2 | async-start | bytes 16777216 | tf_op jit(solution)/shard_map/all_to_all | solution.py:103
  149.0 281.9 %all-reduce.4.cloned.1.call-start = ((), (), s32[]{:S(2)}) async-start(), calls=%async_computation.3 | async-start | bytes 8388608 | tf_op jit(solution)/shard_map/psum | solution.py:14
  295.1 192.8 %all-gather.5.cloned.1.call-start = ((), (), s32[]{:S(2)}) async-start(), calls=%async_computation.4 | async-start | bytes 2359296 | tf_op jit(solution)/shard_map/all_gather | solution.py:138
  432.7 292.6 %all-gather.7.cloned.1.call-start = ((), (), s32[]{:S(2)}) async-start(), calls=%async_computation.5 | async-start | bytes 4718592 | tf_op jit(solution)/shard_map/all_gather | solution.py:153
  495.7 1.0 copy-start.13
  579.1 4.7 copy-start.11
  637.2 6.0 copy-start.3
  655.9 230.9 %all-reduce.6.cloned.1.call-start = ((), (), s32[]{:S(2)}) async-start(), calls=%async_computation.6 | async-start | bytes 8388608 | tf_op jit(solution)/shard_map/psum | solution.py:14
  728.2 2.2 copy-start.1
  730.4 17.0 %copy-start.4 = (f32[2048,512]{1,0:T(8,128)S(1)}, f32[2048,512]{1,0:T(8,128)}, u32[]{:S(2)}) copy-start(f32[2048,512]{1,0:T(8,128)} %all-reduce.4.cloned.1.call-done) | copy-start | bytes 12582916
  730.4 17.0 %copy-start.7 = (f32[2048,512]{1,0:T(8,128)S(1)}, f32[2048,512]{1,0:T(8,128)}, u32[]{:S(2)}) copy-start(f32[2048,512]{1,0:T(8,128)} %gather_fusion.3) | copy-start | bytes 12582916
  730.4 17.1 %copy-start.8 = (f32[2048,512]{1,0:T(8,128)S(1)}, f32[2048,512]{1,0:T(8,128)}, u32[]{:S(2)}) copy-start(f32[2048,512]{1,0:T(8,128)} %get-tuple-element.120) | copy-start | bytes 12582916
  747.4 6.1 copy-start
  753.5 135.2 %copy-start.15 = (s32[4]{0:T(128)S(1)}, s32[4]{0:T(128)}, u32[]{:S(2)}) copy-start(s32[4]{0:T(128)} %constant.489) | copy-start | bytes 52
  753.5 190.0 %all-gather.9.cloned.1.call-start = ((), (), s32[]{:S(2)}) async-start(), calls=%async_computation.7 | async-start | bytes 2359296 | tf_op jit(solution)/shard_map/all_gather | solution.py:138
  888.5 292.6 %all-gather.11.cloned.1.call-start = ((), (), s32[]{:S(2)}) async-start(), calls=%async_computation.8 | async-start | bytes 4718592 | tf_op jit(solution)/shard_map/all_gather | solution.py:153
  951.6 1.1 copy-start.14
  1035.3 5.1 copy-start.12
  1093.0 6.0 copy-start.5
  1184.0 2.2 copy-start.2
  1186.2 17.8 %copy-start.6 = (f32[2048,512]{1,0:T(8,128)S(1)}, f32[2048,512]{1,0:T(8,128)}, u32[]{:S(2)}) copy-start(f32[2048,512]{1,0:T(8,128)} %all-reduce.6.cloned.1.call-done) | copy-start | bytes 12582916
  1186.2 17.8 %copy-start.9 = (f32[2048,512]{1,0:T(8,128)S(1)}, f32[2048,512]{1,0:T(8,128)}, u32[]{:S(2)}) copy-start(f32[2048,512]{1,0:T(8,128)} %gather_fusion.7) | copy-start | bytes 12582916
  1186.2 17.8 %copy-start.10 = (f32[2048,512]{1,0:T(8,128)S(1)}, f32[2048,512]{1,0:T(8,128)}, u32[]{:S(2)}) copy-start(f32[2048,512]{1,0:T(8,128)} %get-tuple-element.124) | copy-start | bytes 12582916
Sparse Core Ops, SparseCore 0:
  295.2 135.7 all-reduce.3
  433.3 54.5 all-gather.4
  656.1 69.1 all-gather.6
  753.7 133.0 all-reduce.5
  889.0 54.5 all-gather.8
  1111.9 69.1 all-gather.10
where the time goes:
time: 1230 us; the launch traced here: 1220 us
  waiting for transfers between devices  658 us (53%)
  other arithmetic  284 us (23%)
  local copies, waits for them, and re-layouts  132 us (11%)
  matrix products  95.1 us (8%)
  starting transfers between devices  27.6 us (2%)
  between operations  19.3 us (2%)
    psum x2, waiting for transfers between devices, from_root(): return lax.psum(kept, axis)  269 us
    another operation x29, other arithmetic, body(): jnp.linalg.cholesky(jnp.tril(diag_block) + jnp.tril(diag_block, -1).T)  159 us
    all_gather x2, waiting for transfers between devices, body(): lax.all_gather(solved_piece, 'tall', axis=0, tiled=True)  115 us
    all_gather x2, waiting for transfers between devices, body(): lax.all_gather(diag_piece, 'tall', axis=0, tiled=True)  107 us
    all_to_all x1, waiting for transfers between devices, body(): lax.all_to_all(buffer, ('wide', 'tall'), split_axis=0, concat_axis=0, til...  90.6 us
    another operation x4, other arithmetic, body(): lax.linalg.triangular_solve(factor, identity, left_side=True, lower=True)  78.7 us
    all_to_all x1, waiting for transfers between devices, relayout(): lax.all_to_all(pieces_out, 'wide', split_axis=2, concat_axis=0, tiled=True)  76.3 us
    dot_general x2, matrix products, body(): jnp.dot(lower_rows, column_rows.T, precision=full_precision, preferred_el...  34.8 us
  transfers between devices with their start and end apart: 9, of which 8 were waited for; matrix products, arithmetic and copies ran while one was open for 6% of the time, Pallas kernels for 0%

commit v1 on v0

--- a/solution.py
+++ b/solution.py
@@ -11,7 +11,7 @@
 
 def from_root(value, axis, source):
     kept = jnp.where(lax.axis_index(axis) == source, value, 0).astype(value.dtype)
-    return lax.psum(kept, axis)
+    return jnp.sum(lax.all_gather(kept, axis), axis=0)
 
 
 def add_blocks(base, tiles, block_index, tile_edge):

time: 1230 us -> 1660 us (1.35)
  waiting for transfers between devices: 658 us -> 1050 us
  other arithmetic: 284 us -> 330 us
    all_gather x0 -> x2, waiting for transfers between devices: none -> 658 us  [from_root(): return jnp.sum(lax.all_gather(kept, axis), axis=0)]
    psum x2 -> x0, waiting for transfers between devices: 269 us -> none  [from_root(): return lax.psum(kept, axis)]
    reduce_sum x0 -> x2, other arithmetic: none -> 46.2 us  [from_root(): return jnp.sum(lax.all_gather(kept, axis), axis=0)]
  transfers between devices with their start and end apart: 9 -> 9, of which waited for: 8 -> 8; matrix products, arithmetic and copies ran while one was open for 6% -> 4% of each run, Pallas kernels for 0% -> 0%
where the time goes in v1:
time: 1660 us; the launch traced here: 1650 us
  waiting for transfers between devices  1050 us (63%)
  other arithmetic  330 us (20%)
  local copies, waits for them, and re-layouts  133 us (8%)
  matrix products  95.1 us (6%)
  starting transfers between devices  27.6 us (2%)
  between operations  19.5 us (1%)
    all_gather x2, waiting for transfers between devices, from_root(): return jnp.sum(lax.all_gather(kept, axis), axis=0)  658 us
    another operation x29, other arithmetic, body(): jnp.linalg.cholesky(jnp.tril(diag_block) + jnp.tril(diag_block, -1).T)  159 us
    all_gather x2, waiting for transfers between devices, body(): lax.all_gather(solved_piece, 'tall', axis=0, tiled=True)  114 us
    all_gather x2, waiting for transfers between devices, body(): lax.all_gather(diag_piece, 'tall', axis=0, tiled=True)  106 us
    all_to_all x1, waiting for transfers between devices, body(): lax.all_to_all(buffer, ('wide', 'tall'), split_axis=0, concat_axis=0, til...  90.6 us
    another operation x4, other arithmetic, body(): lax.linalg.triangular_solve(factor, identity, left_side=True, lower=True)  78.7 us
    all_to_all x1, waiting for transfers between devices, relayout(): lax.all_to_all(pieces_out, 'wide', split_axis=2, concat_axis=0, tiled=True)  76.3 us
    reduce_sum x2, other arithmetic, from_root(): return jnp.sum(lax.all_gather(kept, axis), axis=0)  46.2 us
  transfers between devices with their start and end apart: 9, of which 8 were waited for; matrix products, arithmetic and copies ran while one was open for 4% of the time, Pallas kernels for 0%

profile of v1, /device:TPU:1, one launch (start us, length us, event | category | flops | bytes accessed | tf_op | source)
XLA Modules:
  0.0 1650.7 jit_solution(2472410711079009400)
XLA Ops:
  8.9 11.5 all-to-all-start.1
  20.4 9.9 copy.64
  30.2 9.5 copy.39
  39.7 6.5 all-to-all-start
  46.2 8.4 convolution_bitcast_fusion
  54.5 9.8 copy.41
  64.4 76.3 %all-to-all-done = f32[128,2,16,512]{3,1,0,2:T(2,128)} async-done(((f32[128,2,16,512]{3,1,0,2:T(2,128)}), f32[128,2,16,512]{3,1,0,2:T(2,128)}, u32[]{:S(2)}, u32[]{:S(2)}) %all-to-all-start) | async-done | bytes 8388640 | tf_op jit(solution)/shard_map/all_to_all | solution.py:32
  140.6 8.4 all-to-all-start.2
  149.5 8.9 copy.65
  158.3 90.6 %all-to-all-done.2 = f32[128,1,16384]{2,1,0:T(1,128)} async-done(((f32[128,1,16384]{2,1,0:T(1,128)}), f32[128,1,16384]{2,1,0:T(1,128)}, u32[]{:S(2)}, u32[]{:S(2)}) %all-to-all-start.2) | async-done | bytes 8388640 | tf_op jit(solution)/shard_map/all_to_all | solution.py:103
  248.9 18.0 %copy.63 = f32[128,1,16384]{0,2,1:T(8,128)} copy(f32[128,1,16384]{2,1,0:T(1,128)} %all-to-all-done.2) | data formatting | bytes 16777216 | tf_op jit(solution)/shard_map/dot_general | solution.py:23
  266.9 11.2 fusion.82
  278.1 12.3 bitcast_add_fusion
  290.4 4.7 slice_select_fusion
  295.1 330.1 %all-gather.17.cloned.1.call-done = f32[32768,512]{1,0:T(8,128)} async-done(((f32[2048,512]{1,0:T(8,128)}), f32[32768,512]{1,0:T(8,128)}) %all-gather.17.cloned.1.call-update) | async-done | bytes 67108880 | tf_op jit(solution)/shard_map/all_gather | solution.py:14
  625.2 23.1 %reduce_sum.31 = f32[2048,512]{1,0:T(8,128)} reduce(f32[16,2048,512]{2,1,0:T(8,128)} %bitcast.12, f32[]{:T(128)} %constant.398.clone.1), dimensions={0}, to_apply=%region_2.3 | reduce | flops 15728640 | bytes 71303168 | tf_op jit(solution)/shard_map/reduce_sum | solution.py:14
  651.8 52.3 %all-gather.9.cloned.1.call-done = f32[8,128,512]{2,1,0:T(8,128)} async-done(((f32[1,128,512]{2,1,0:T(8,128)}), f32[8,128,512]{2,1,0:T(8,128)}) %all-gather.9.cloned.1.call-update) | async-done | bytes 2097168 | tf_op jit(solution)/shard_map/all_gather | solution.py:138
  704.1 2.2 gather_fusion
  713.0 11.7 cholesky.286
  724.9 9.8 custom-call.27
  737.2 11.8 cholesky.305
  749.1 9.8 custom-call.28
  760.5 11.7 cholesky.326
  772.2 9.8 custom-call.29
  783.5 11.9 cholesky.343
  800.1 2.5 fusion.25
  802.6 11.3 while.7
  803.2 2.2 bitcast_dynamic-update-slice_fusion.4
  806.1 2.2 bitcast_dynamic-update-slice_fusion.4
  808.9 2.2 bitcast_dynamic-update-slice_fusion.4
  813.9 39.3 %custom-call.30 = f32[4,128,128]{1,2,0:T(8,128)S(1)} custom-call(f32[4,128,128]{2,1,0:T(8,128)S(1)} %get-tuple-element.61), custom_call_target="InvertDiagBlocksLowerTriangular" | custom-call | tf_op jit(solution)/shard_map/triangular_solve/custom-call.3 | solution.py:141
  859.3 8.9 broadcast_select_fusion.2
  868.2 2.8 gather_fusion.1
  873.8 9.0 gather_fusion.3
  882.7 58.5 %all-gather.11.cloned.1.call-done = f32[16,128,512]{2,1,0:T(8,128)} async-done(((f32[2,128,512]{2,1,0:T(8,128)}), f32[16,128,512]{2,1,0:T(8,128)}) %all-gather.11.cloned.1.call-update) | async-done | bytes 4194320 | tf_op jit(solution)/shard_map/all_gather | solution.py:153
  941.3 2.9 gather_fusion.2
  946.3 17.0 %convolution_subtract_fusion.1 = f32[2048,1024]{1,0:T(8,128)S(1)} fusion(f32[2048,1024]{1,0:T(8,128)} %bitcast_add_fusion, f32[2048,512]{1,0:T(8,128)S(1)} %copy-done.5, f32[1024,512]{1,0:T(8,128)S(1)} %bitcast.193), kind=kOutput, calls=%fused_computation.25 | convolution fusion | flops 12886999040 | bytes 23068672 | tf_op jit(solution)/shard_map/dot_general | solution.py:158
  963.4 6.0 broadcast_select_fusion.1
  969.5 327.5 %all-gather.19.cloned.1.call-done = f32[32768,512]{1,0:T(8,128)} async-done(((f32[2048,512]{1,0:T(8,128)}), f32[32768,512]{1,0:T(8,128)}) %all-gather.19.cloned.1.call-update) | async-done | bytes 67108880 | tf_op jit(solution)/shard_map/all_gather | solution.py:14
  1297.0 23.1 %reduce_sum.32 = f32[2048,512]{1,0:T(8,128)} reduce(f32[16,2048,512]{2,1,0:T(8,128)} %bitcast.31, f32[]{:T(128)} %constant.398.clone.1), dimensions={0}, to_apply=%region_12.20 | reduce | flops 15728640 | bytes 71303168 | tf_op jit(solution)/shard_map/reduce_sum | solution.py:14
  1322.1 53.9 %all-gather.13.cloned.1.call-done = f32[8,128,512]{2,1,0:T(8,128)} async-done(((f32[1,128,512]{2,1,0:T(8,128)}), f32[8,128,512]{2,1,0:T(8,128)}) %all-gather.13.cloned.1.call-update) | async-done | bytes 2097168 | tf_op jit(solution)/shard_map/all_gather | solution.py:138
  1376.0 2.2 gather_fusion.4
  1384.8 11.7 cholesky.358
  1396.7 9.8 custom-call.31
  1409.0 11.7 cholesky.377
  1420.8 10.0 custom-call.32
  1432.4 11.7 cholesky.398
  1444.1 9.8 custom-call.33
  1455.4 12.1 cholesky.415
  1472.9 2.5 fusion.22
  1475.3 11.7 while.8
  1476.0 2.3 bitcast_dynamic-update-slice_fusion.5
  1479.0 2.3 bitcast_dynamic-update-slice_fusion.5
  1481.9 2.3 bitcast_dynamic-update-slice_fusion.5
  1484.9 2.2 bitcast_dynamic-update-slice_fusion.5
  1487.1 39.3 %custom-call.34 = f32[4,128,128]{1,2,0:T(8,128)S(1)} custom-call(f32[4,128,128]{2,1,0:T(8,128)S(1)} %get-tuple-element.62), custom_call_target="InvertDiagBlocksLowerTriangular" | custom-call | tf_op jit(solution)/shard_map/triangular_solve/custom-call.3 | solution.py:141
  1532.4 8.9 broadcast_select_fusion
  1541.4 2.8 gather_fusion.5
  1545.2 4.6 constant_dynamic-update-slice_fusion.6
  1549.8 8.9 gather_fusion.7
  1558.8 55.7 %all-gather.15.cloned.1.call-done = f32[16,128,512]{2,1,0:T(8,128)} async-done(((f32[2,128,512]{2,1,0:T(8,128)}), f32[16,128,512]{2,1,0:T(8,128)}) %all-gather.15.cloned.1.call-update) | async-done | bytes 4194320 | tf_op jit(solution)/shard_map/all_gather | solution.py:153
  1614.5 2.9 gather_fusion.6
  1619.5 17.8 %convolution_subtract_fusion = f32[2048,1024]{1,0:T(8,128)} fusion(f32[2048,1024]{1,0:T(8,128)} %constant_dynamic-update-slice_fusion.6, f32[2048,512]{1,0:T(8,128)S(1)} %copy-done.6, f32[1024,512]{1,0:T(8,128)S(1)} %bitcast.192), kind=kOutput, calls=%fused_computation.24 | convolution fusion | flops 12886999040 | bytes 23068672 | tf_op jit(solution)/shard_map/dot_general | solution.py:158
  1637.3 6.4 fusion
  (157 shorter events, 65.4 us)
Async XLA Ops:
  8.9 30.9 %all-to-all-start.1 = ((s32[128,1,2]{2,1,0:T(1,128)}), s32[128,1,2]{2,1,0:T(1,128)S(1)}, u32[]{:S(2)}, u32[]{:S(2)}) async-start(s32[128,1,2]{2,1,0:T(1,128)} %copy.40), calls=%async_computation.1 | async-start | bytes 131072 | tf_op jit(solution)/shard_map/all_to_all | solution.py:104
  39.7 100.9 %all-to-all-start = ((f32[128,2,16,512]{3,1,0,2:T(2,128)}), f32[128,2,16,512]{3,1,0,2:T(2,128)}, u32[]{:S(2)}, u32[]{:S(2)}) async-start(f32[128,2,16,512]{3,1,0,2:T(2,128)} %copy.39), calls=%async_computation | async-start | bytes 16777216 | tf_op jit(solution)/shard_map/all_to_all | solution.py:32
  140.6 108.2 %all-to-all-start.2 = ((f32[128,1,16384]{2,1,0:T(1,128)}), f32[128,1,16384]{2,1,0:T(1,128)}, u32[]{:S(2)}, u32[]{:S(2)}) async-start(f32[128,1,16384]{2,1,0:T(1,128)} %copy.41), calls=%async_computation.2 | async-start | bytes 16777216 | tf_op jit(solution)/shard_map/all_to_all | solution.py:103
  149.0 476.1 %all-gather.17.cloned.1.call-start = ((), (), s32[]{:S(2)}) async-start(), calls=%async_computation.7 | async-start | bytes 71303168 | tf_op jit(solution)/shard_map/all_gather | solution.py:14
  295.1 409.1 %all-gather.9.cloned.1.call-start = ((), (), s32[]{:S(2)}) async-start(), calls=%async_computation.3 | async-start | bytes 2359296 | tf_op jit(solution)/shard_map/all_gather | solution.py:138
  650.0 291.3 %all-gather.11.cloned.1.call-start = ((), (), s32[]{:S(2)}) async-start(), calls=%async_computation.4 | async-start | bytes 4718592 | tf_op jit(solution)/shard_map/all_gather | solution.py:153
  712.0 1.0 copy-start.13
  795.4 4.7 copy-start.11
  853.2 6.1 copy-start.1
  871.9 425.1 %all-gather.19.cloned.1.call-start = ((), (), s32[]{:S(2)}) async-start(), calls=%async_computation.8 | async-start | bytes 71303168 | tf_op jit(solution)/shard_map/all_gather | solution.py:14
  944.2 2.2 copy-start.5
  946.3 17.0 %copy-start.2 = (f32[2048,512]{1,0:T(8,128)S(1)}, f32[2048,512]{1,0:T(8,128)}, u32[]{:S(2)}) copy-start(f32[2048,512]{1,0:T(8,128)} %reduce_sum.31) | copy-start | bytes 12582916
  946.3 17.0 %copy-start.7 = (f32[2048,512]{1,0:T(8,128)S(1)}, f32[2048,512]{1,0:T(8,128)}, u32[]{:S(2)}) copy-start(f32[2048,512]{1,0:T(8,128)} %gather_fusion.3) | copy-start | bytes 12582916
  946.3 17.1 %copy-start.8 = (f32[2048,512]{1,0:T(8,128)S(1)}, f32[2048,512]{1,0:T(8,128)}, u32[]{:S(2)}) copy-start(f32[2048,512]{1,0:T(8,128)} %get-tuple-element.120) | copy-start | bytes 12582916
  963.4 6.0 copy-start
  969.4 406.6 %all-gather.13.cloned.1.call-start = ((), (), s32[]{:S(2)}) async-start(), calls=%async_computation.5 | async-start | bytes 2359296 | tf_op jit(solution)/shard_map/all_gather | solution.py:138
  1297.0 25.0 %copy-start.15 = (s32[4]{0:T(128)S(1)}, s32[4]{0:T(128)}, u32[]{:S(2)}) copy-start(s32[4]{0:T(128)} %constant.489) | copy-start | bytes 52
  1321.8 292.7 %all-gather.15.cloned.1.call-start = ((), (), s32[]{:S(2)}) async-start(), calls=%async_computation.6 | async-start | bytes 4718592 | tf_op jit(solution)/shard_map/all_gather | solution.py:153
  1383.8 1.0 copy-start.14
  1467.5 5.4 copy-start.12
  1526.4 6.1 copy-start.3
  1617.3 2.2 copy-start.6
  1619.5 17.8 %copy-start.4 = (f32[2048,512]{1,0:T(8,128)S(1)}, f32[2048,512]{1,0:T(8,128)}, u32[]{:S(2)}) copy-start(f32[2048,512]{1,0:T(8,128)} %reduce_sum.32) | copy-start | bytes 12582916
  1619.5 17.8 %copy-start.9 = (f32[2048,512]{1,0:T(8,128)S(1)}, f32[2048,512]{1,0:T(8,128)}, u32[]{:S(2)}) copy-start(f32[2048,512]{1,0:T(8,128)} %gather_fusion.7) | copy-start | bytes 12582916
  1619.5 17.8 %copy-start.10 = (f32[2048,512]{1,0:T(8,128)S(1)}, f32[2048,512]{1,0:T(8,128)}, u32[]{:S(2)}) copy-start(f32[2048,512]{1,0:T(8,128)} %get-tuple-element.124) | copy-start | bytes 12582916
Sparse Core Ops, SparseCore 0:
  295.2 329.9 all-gather.16
  650.1 54.0 all-gather.8
  872.0 69.1 all-gather.10
  969.5 327.4 all-gather.18
  1321.9 54.0 all-gather.12
  1545.2 69.1 all-gather.14
